TPU v7x, 32 devices: a whole 2x2x4 slice. The times are simulated.
32 devices in a mesh: groups: 2 (over y), ctx: 4 (over z), head: 2 (over x), pair: 2 (over core).
Axes of the slice: x: 2, y: 2, z: 4, core: 2. Of those that a mesh axis runs over, the one named last changes fastest.
Arguments:
- student_query: bfloat16 [1024, 4096], P(('groups', 'ctx'), ('head', 'pair')), parts along dimension 0, may hold values from -25 to 25
- teacher_keys: bfloat16 [1024, 1024], P(('groups', 'ctx'), ('head', 'pair')), parts along dimension 0, may hold values from -9 to 9
- teacher_values: bfloat16 [1024, 1024], P(('groups', 'ctx'), ('head', 'pair')), parts along dimension 0, may hold values from -6 to 6
- band_span: int32 [1024], P(('groups', 'ctx')), parts along dimension 0, may hold values from 256 to 1024, as said below
- residual_in: bfloat16 [1024, 4096], P(('groups', 'ctx'), ('head', 'pair')), parts along dimension 0, may hold values from -3 to 3
- norm_gain: float32 [4096], replicated, may hold values from 0.25 to 1.75
- w_gate: bfloat16 [4096, 7168], P('ctx', ('head', 'pair')), may hold values from -0.09375 to 0.09375
- w_up: bfloat16 [4096, 7168], P('ctx', ('head', 'pair')), may hold values from -0.09375 to 0.09375
- w_down: bfloat16 [7168, 4096], P(('head', 'pair'), 'ctx'), may hold values from -0.0625 to 0.0625
- teacher_feats: bfloat16 [1024, 7168], P(('groups', 'ctx'), ('head', 'pair')), parts along dimension 0, may hold values from -31 to 31
- keep_tiles: int32 [1024, 56], P(('groups', 'ctx'), ('head', 'pair')), parts along dimension 0, may hold values from 0 to 1, as said below
Outputs:
- layer_out: bfloat16 [1024, 4096], P(('groups', 'ctx'), ('head', 'pair')), parts along dimension 0
- loss_value: float32 [2], P('groups'), parts along dimension 0
- grad_resid: float32 [1024, 4096], P(('groups', 'ctx'), ('head', 'pair')), parts along dimension 0
There are 2 independent parts, one for each index of `groups`. A program takes and returns all parts, laid end to end along the dimension named above; an argument that names none is the same for every part. Nothing has to cross between parts.
Inputs may be any that keep to these rules, and one draw needn't show every extreme that they name: `band_span`: some token's span equals 1024. `keep_tiles`: the first token keeps every tile.
All inputs are finite; a program needn't handle non-finite values.
Results may differ from a plain program's by a relative error of at most 0.014.
Values may be sent and summed in bfloat16 or wider, within the bound.
No kernel may reach another device: no remote copies, remote signals or barrier semaphores. Data moves between devices by JAX's collectives and lax.ppermute only.
A program may use at most 128 MiB of HBM per device.

v0:
```python
import math
import jax
import jax.numpy as jnp
from jax import lax
from jax.sharding import PartitionSpec as P

D = 4096
HEADS = 32
KV_HEADS = 8
HEAD_DIM = 128
TILE = 128
BAND = 8


def passed_along(block, axis, distance):
    devices = range(lax.axis_size(axis))
    route = [(i - distance, i) for i in devices if i - distance in devices]
    return lax.ppermute(block, axis, route)


def attend_heads(query_part, key_rows, value_rows, allowed):
    scores = jnp.einsum("thd,sd->hts", query_part, key_rows, preferred_element_type=jnp.float32) * (
        1.0 / math.sqrt(HEAD_DIM)
    )
    masked = jnp.where(allowed[None], scores, -jnp.inf)
    highest = jnp.max(masked, axis=-1, keepdims=True)
    weights = jnp.exp(masked - highest)
    normalized = (weights / jnp.sum(weights, axis=-1, keepdims=True)).astype(jnp.bfloat16)
    return jnp.einsum("hts,sd->thd", normalized, value_rows, preferred_element_type=jnp.float32)


def local(
    student_query,
    teacher_keys,
    teacher_values,
    band_span,
    residual_in,
    norm_gain,
    w_gate,
    w_up,
    w_down,
    teacher_feats,
    keep_tiles,
):
    tok_rows = student_query.shape[0]
    kv_local = teacher_keys.shape[1] // HEAD_DIM
    group_size = HEADS // KV_HEADS
    ctx_index = lax.axis_index("ctx")
    paired = jnp.stack([teacher_keys, teacher_values])

    def pass_block(carried, unused_step):
        moved = passed_along(carried, "ctx", 1)
        return (moved, moved)

    unused_last, earlier = lax.scan(pass_block, paired, None, length=BAND)
    all_blocks = jnp.concatenate([paired[None], earlier], axis=0)
    rounds_count = BAND + 1
    round_ids = jnp.arange(rounds_count, dtype=jnp.int32)
    key_pos = (
        (ctx_index - round_ids)[:, None] * tok_rows + jnp.arange(tok_rows, dtype=jnp.int32)[None, :]
    ).reshape(-1)
    query_pos = ctx_index * tok_rows + jnp.arange(tok_rows, dtype=jnp.int32)
    distance = query_pos[:, None] - key_pos[None, :]
    allowed = (distance >= 0) & (distance < band_span[:, None]) & (key_pos[None, :] >= 0)
    keys_flat = all_blocks[:, 0].reshape(rounds_count * tok_rows, kv_local, HEAD_DIM)
    values_flat = all_blocks[:, 1].reshape(rounds_count * tok_rows, kv_local, HEAD_DIM)
    query_heads = student_query.reshape(tok_rows, kv_local, group_size, HEAD_DIM)
    outputs = []
    for kv_head in range(kv_local):
        for first_head in range(0, group_size, 2):
            outputs.append(
                attend_heads(
                    query_heads[:, kv_head, first_head : first_head + 2],
                    keys_flat[:, kv_head],
                    values_flat[:, kv_head],
                    allowed,
                )
            )
    attended = jnp.concatenate(outputs, axis=1).reshape(tok_rows, -1)
    residual = (residual_in.astype(jnp.float32) + attended).astype(jnp.bfloat16)
    gathered = lax.all_gather(residual, ("head", "pair"), axis=1, tiled=True)
    full_float = gathered.astype(jnp.float32)
    rms_value = jnp.sqrt(jnp.mean(full_float * full_float, axis=1, keepdims=True) + 1e-05)
    normed = (full_float / rms_value * norm_gain).astype(jnp.bfloat16)
    gate_full, up_full = (
        lax.all_gather(w_gate, "ctx", axis=0, tiled=True),
        lax.all_gather(w_up, "ctx", axis=0, tiled=True),
    )
    gate_proj = jnp.dot(normed, gate_full, preferred_element_type=jnp.float32)
    up_proj = jnp.dot(normed, up_full, preferred_element_type=jnp.float32)
    lifted = jnp.maximum(gate_proj, 0.0)
    squared = lifted * lifted
    act_value = squared * up_proj
    hidden = act_value.astype(jnp.bfloat16)
    all_hidden = lax.all_gather(hidden, "ctx", axis=0, tiled=True)
    local_part = jnp.dot(all_hidden, w_down, preferred_element_type=jnp.float32).astype(
        jnp.bfloat16
    )
    routed = lax.all_to_all(local_part, "ctx", split_axis=0, concat_axis=1, tiled=True)
    down_sum = lax.psum_scatter(
        routed.astype(jnp.float32).astype(jnp.bfloat16),
        ("head", "pair"),
        scatter_dimension=1,
        tiled=True,
    ).astype(jnp.float32)
    resid_own = residual.astype(jnp.float32)
    layer_out = (resid_own + down_sum).astype(jnp.bfloat16)
    tile_count = keep_tiles.shape[1]
    keep_float = keep_tiles.astype(jnp.float32)
    keep_wide = jnp.broadcast_to(keep_float[:, :, None], (tok_rows, tile_count, TILE)).reshape(
        tok_rows, tile_count * TILE
    )
    differ = act_value - teacher_feats.astype(jnp.float32)
    loss_part = jnp.sum(keep_wide * differ * differ)
    count_part = jnp.sum(keep_float) * TILE
    loss_total, count_total = lax.psum((loss_part, count_part), ("ctx", "head", "pair"))
    loss_value = (loss_total / count_total).reshape(1)
    grad_act = keep_wide * differ
    grad_gate = (grad_act * up_proj * 2.0 * lifted).astype(jnp.bfloat16)
    grad_up = (grad_act * squared).astype(jnp.bfloat16)
    contract = (((1,), (1,)), ((), ()))
    grad_part = lax.dot_general(grad_gate, gate_full, contract, preferred_element_type=jnp.float32)
    grad_part = grad_part + lax.dot_general(
        grad_up, up_full, contract, preferred_element_type=jnp.float32
    )
    own_cols = residual.shape[1]
    own_start = lax.axis_index(("head", "pair")) * own_cols
    gain_own = lax.dynamic_slice_in_dim(norm_gain, own_start, own_cols, 0)
    rms_cubed = rms_value * rms_value * rms_value
    grad_norm = lax.psum_scatter(
        grad_part.astype(jnp.bfloat16), ("head", "pair"), scatter_dimension=1, tiled=True
    ).astype(jnp.float32)
    inner_sum = lax.psum(
        jnp.sum(gain_own * grad_norm * resid_own, axis=1, keepdims=True), ("head", "pair")
    )
    grad_resid = gain_own * grad_norm / rms_value - resid_own * inner_sum / (D * rms_cubed)
    return (layer_out, loss_value, grad_resid)


def solution(mesh):
    in_specs = (
        P(("groups", "ctx"), ("head", "pair")),
        P(("groups", "ctx"), ("head", "pair")),
        P(("groups", "ctx"), ("head", "pair")),
        P(("groups", "ctx")),
        P(("groups", "ctx"), ("head", "pair")),
        P(),
        P("ctx", ("head", "pair")),
        P("ctx", ("head", "pair")),
        P(("head", "pair"), "ctx"),
        P(("groups", "ctx"), ("head", "pair")),
        P(("groups", "ctx"), ("head", "pair")),
    )
    out_specs = (
        P(("groups", "ctx"), ("head", "pair")),
        P("groups"),
        P(("groups", "ctx"), ("head", "pair")),
    )
    return jax.shard_map(local, mesh=mesh, in_specs=in_specs, out_specs=out_specs, check_vma=False)
```

profile of v0, /device:TPU:0, one launch (start us, length us, event | category | flops | bytes accessed | tf_op | source)
XLA Modules:
  0.0 737.4 jit_solution(9024494652574293018)
XLA Ops:
  7.2 0.1 add_bitcast_fusion
  7.3 0.1 broadcast_compare_fusion
  7.4 0.9 fusion.71
  8.3 57.8 %while.12 = (s32[]{:T(128)}, bf16[2,128,256]{2,1,0:T(8,128)(2,1)S(1)}, bf16[8,2,128,256]{3,2,1,0:T(8,128)(2,1)S(1)}, s32[]{:T(128)}) while((s32[]{:T(128)}, bf16[2,128,256]{2,1,0:T(8,128)(2,1)S(1)}, bf16[8,2,128,256]{3,2,1,0:T(8,128)(2,1)S(1)}, s32[]{:T(128)}) %tuple.30), condition=%wide.region_1.2_spmd, body=%wide.region_0.1_spmd.sunk | while | flops 2 | bytes 1048681 | solution.py:55
  8.3 5.0 collective-permute-start
  13.3 2.7 collective-permute-done
  16.0 4.4 collective-permute-start
  20.4 2.5 collective-permute-done
  23.0 4.4 collective-permute-start
  27.4 2.5 collective-permute-done
  29.9 4.4 collective-permute-start
  34.3 2.5 collective-permute-done
  36.8 4.4 collective-permute-start
  41.2 3.5 collective-permute-done
  44.8 4.4 collective-permute-start
  49.2 3.0 collective-permute-done
  52.3 4.4 collective-permute-start
  56.7 2.5 collective-permute-done
  59.2 4.4 collective-permute-start
  63.6 2.5 collective-permute-done
  66.1 0.1 fusion.25
  66.2 0.1 reshape_squeeze.7
  66.4 0.9 fusion.76
  67.3 0.1 copy-done.4
  67.3 0.2 copy.24
  67.5 0.9 fusion.27
  68.4 0.6 fusion.80
  69.0 0.6 fusion.79
  69.6 0.6 fusion.78
  70.2 0.6 fusion.77
  70.8 0.1 reshape_squeeze.6
  70.9 0.9 fusion.75
  71.8 0.6 copy.42
  72.5 0.8 convolution_bitcast_fusion.3
  73.3 0.8 convolution_bitcast_fusion.2
  74.1 0.6 copy.46
  74.7 0.8 convolution_bitcast_fusion.1
  75.5 0.8 convolution_bitcast_fusion
  76.4 0.2 copy.35
  76.6 0.7 copy-done.5
  77.3 0.8 add_convert_fusion
  78.1 0.7 all-gather.7.cloned.1.call-update
  78.9 0.7 all-gather.9.cloned.1.call-update
  79.6 0.2 all-gather.11.cloned.1.call-start
  79.8 0.1 broadcast_in_dim.67
  79.9 0.3 copy.37
  80.2 16.9 %all-gather.5.cloned.1.call-done = bf16[128,4096]{1,0:T(8,128)(2,1)} async-done(((bf16[128,1024]{1,0:T(8,128)(2,1)}), bf16[128,4096]{1,0:T(8,128)(2,1)}) %all-gather.5.cloned.1.call-update) | async-done | bytes 1048592 | tf_op jit(solution)/shard_map/all_gather | solution.py:81
  97.1 1.5 fusion.21
  98.6 252.5 %all-gather.7.cloned.1.call-done = bf16[4096,1792]{1,0:T(8,128)(2,1)} async-done(((bf16[1024,1792]{1,0:T(8,128)(2,1)}), bf16[4096,1792]{1,0:T(8,128)(2,1)}) %all-gather.7.cloned.1.call-update) | async-done | bytes 14680080 | tf_op jit(solution)/shard_map/all_gather | solution.py:86
  351.1 7.7 %convolution_maximum_fusion = f32[128,1792]{1,0:T(8,128)S(1)} fusion(bf16[4096,1792]{1,0:T(8,128)(2,1)} %all-gather.7.cloned.1.call-done, bf16[128,4096]{1,0:T(8,128)(2,1)} %all-gather.5.cloned.1.call-done, f32[4096]{0:T(1024)S(1)} %copy-done.7, f32[128]{0:T(128)S(1)} %get-tuple-element.42), kind=kOutput, calls=%fused_computation.29 | convolution fusion | flops 1881374720 | bytes 16663040 | tf_op jit(solution)/shard_map/dot_general | solution.py:89
  358.9 244.5 %all-gather.9.cloned.1.call-done = bf16[4096,1792]{1,0:T(8,128)(2,1)} async-done(((bf16[1024,1792]{1,0:T(8,128)(2,1)}), bf16[4096,1792]{1,0:T(8,128)(2,1)}) %all-gather.9.cloned.1.call-update) | async-done | bytes 14680080 | tf_op jit(solution)/shard_map/all_gather | solution.py:87
  603.4 9.0 %multiply_reduce_fusion = (f32[]{:T(128)}, bf16[128,1792]{1,0:T(8,128)(2,1)}, f32[128,1792]{1,0:T(8,128)}) fusion(bf16[128,1792]{1,0:T(8,128)(2,1)S(1)} %copy-done.2, f32[128,1792]{1,0:T(8,128)S(1)} %copy.37, f32[128,1792]{1,0:T(8,128)S(1)} %convolution_maximum_fusion, bf16[4096,1792]{1,0:T(8,128)(2,1)} %all-gather.9.cloned.1.call-done, ...), kind=kOutput, calls=%fused_computation.46 | convolution fusion | flops 1882980352 | bytes 19415556 | tf_op jit(solution)/shard_map/dot_general | solution.py:90
  612.5 0.0 reduce-scatter.5.cloned.1.call-start
  612.5 10.8 %fusion.32 = f32[128,4096]{1,0:T(8,128)S(1)} fusion(bf16[4096,1792]{1,0:T(8,128)(2,1)} %all-gather.7.cloned.1.call-done, f32[128,1792]{1,0:T(8,128)} %copy-done.1, f32[128,1792]{1,0:T(8,128)} %get-tuple-element.43, f32[128,1792]{1,0:T(8,128)S(1)} %copy.37, bf16[128,1792]{1,0:T(8,128)(2,1)S(1)} %copy-done.2), kind=kOutput, calls=%fused_computation.66 | convolution fusion | flops 1881112576 | bytes 19988480 | tf_op jit(solution)/shard_map/dot_general | solution.py:122
  623.3 11.6 %fusion.4 = bf16[128,4096]{1,0:T(8,128)(2,1)} fusion(f32[128,4096]{1,0:T(8,128)S(1)} %fusion.32, bf16[4096,1792]{1,0:T(8,128)(2,1)} %all-gather.9.cloned.1.call-done, f32[128,1792]{1,0:T(8,128)} %copy-done.1, f32[128,1792]{1,0:T(8,128)S(1)} %copy.37, bf16[128,1792]{1,0:T(8,128)(2,1)S(1)} %copy-done.2, f32[128,1792]{1,0:T(8,128)} %get-tuple-element.43), kind=kOutput, calls=%fused_computation.6 | convolution fusion | flops 1881702400 | bytes 21037056 | tf_op jit(solution)/shard_map/dot_general | solution.py:123
  635.0 17.2 %all-gather.11.cloned.1.call-done = bf16[512,1792]{1,0:T(8,128)(2,1)} async-done(((bf16[128,1792]{1,0:T(8,128)(2,1)}), bf16[512,1792]{1,0:T(8,128)(2,1)}) %all-gather.11.cloned.1.call-update) | async-done | bytes 1835024 | tf_op jit(solution)/shard_map/all_gather | solution.py:95
  652.1 4.7 convolution_convert_fusion
  656.8 28.1 %all_to_all.19 = bf16[4,128,1024]{2,1,0:T(8,128)(2,1)S(1)} all-to-all(bf16[4,128,1024]{2,1,0:T(8,128)(2,1)S(1)} %bitcast.216), channel_id=1, replica_groups=mesh['groups'=2,'ctx'=4,'head'=2,'pair'=2] {'ctx'}, dimensions={0} | all-to-all | bytes 2097152 | tf_op jit(solution)/shard_map/all_to_all | solution.py:99
  684.9 1.1 copy.50
  686.1 0.6 convert_reduce_fusion
  687.3 31.7 %all-reduce = (f32[]{:T(128)}, f32[]{:T(128)}) all-reduce(f32[]{:T(128)} %get-tuple-element.29, f32[]{:T(128)S(6)} %mul.149), channel_id=1, replica_groups=mesh['groups'=2,'ctx'=4,'head'=2,'pair'=2] {'ctx','head','pair'}, use_global_device_ids=true, to_apply=%region_13.14 | all-reduce | flops 2 | bytes 16 | tf_op jit(solution)/shard_map/psum | solution.py:116
  720.4 1.1 fusion.29
  721.5 5.8 psum.23
  727.3 2.1 fusion.31
  (49 shorter events, 0.6 us)
Async XLA Ops:
  7.2 89.9 %all-gather.5.cloned.1.call-start = ((), (), s32[]{:S(2)}) async-start(), calls=%async_computation.3 | async-start | bytes 1310720 | tf_op jit(solution)/shard_map/all_gather | solution.py:81
  8.3 7.7 %collective-permute-start = (bf16[2,128,256]{2,1,0:T(8,128)(2,1)S(1)}, bf16[2,128,256]{2,1,0:T(8,128)(2,1)S(1)}, u32[]{:S(2)}, u32[]{:S(2)}) collective-permute-start(bf16[2,128,256]{2,1,0:T(8,128)(2,1)S(1)} %get-tuple-element.68), channel_id=1, source_target_pairs={{0,4},{4,8},{8,12},{1,5},{5,9},{9,13},{2,6},{6,10},{10,14},{3,7},{... | collective-permute-start | bytes 393224 | tf_op jit(solution)/shard_map/while/body/eval_jaxpr/ppermute | solution.py:18
  16.0 6.9 collective-permute-start
  23.0 6.9 collective-permute-start
  29.9 6.9 collective-permute-start
  36.8 7.9 %collective-permute-start = (bf16[2,128,256]{2,1,0:T(8,128)(2,1)S(1)}, bf16[2,128,256]{2,1,0:T(8,128)(2,1)S(1)}, u32[]{:S(2)}, u32[]{:S(2)}) collective-permute-start(bf16[2,128,256]{2,1,0:T(8,128)(2,1)S(1)} %get-tuple-element.68), channel_id=1, source_target_pairs={{0,4},{4,8},{8,12},{1,5},{5,9},{9,13},{2,6},{6,10},{10,14},{3,7},{... | collective-permute-start | bytes 393224 | tf_op jit(solution)/shard_map/while/body/eval_jaxpr/ppermute | solution.py:18
  44.8 7.4 %collective-permute-start = (bf16[2,128,256]{2,1,0:T(8,128)(2,1)S(1)}, bf16[2,128,256]{2,1,0:T(8,128)(2,1)S(1)}, u32[]{:S(2)}, u32[]{:S(2)}) collective-permute-start(bf16[2,128,256]{2,1,0:T(8,128)(2,1)S(1)} %get-tuple-element.68), channel_id=1, source_target_pairs={{0,4},{4,8},{8,12},{1,5},{5,9},{9,13},{2,6},{6,10},{10,14},{3,7},{... | collective-permute-start | bytes 393224 | tf_op jit(solution)/shard_map/while/body/eval_jaxpr/ppermute | solution.py:18
  52.3 6.9 collective-permute-start
  59.2 6.9 collective-permute-start
  66.4 1.0 copy-start.4
  66.4 1.1 copy-start.8
  76.3 1.0 copy-start.5
  78.1 273.1 %all-gather.7.cloned.1.call-start = ((), (), s32[]{:S(2)}) async-start(), calls=%async_computation.4 | async-start | bytes 18350080 | tf_op jit(solution)/shard_map/all_gather | solution.py:86
  78.8 1.0 copy-start.6
  78.8 524.6 %all-gather.9.cloned.1.call-start = ((), (), s32[]{:S(2)}) async-start(), calls=%async_computation.5 | async-start | bytes 18350080 | tf_op jit(solution)/shard_map/all_gather | solution.py:87
  79.6 572.6 %all-gather.11.cloned.1.call-start = ((), (), s32[]{:S(2)}) async-start(), calls=%async_computation.6 | async-start | bytes 2293760 | tf_op jit(solution)/shard_map/all_gather | solution.py:95
  79.9 271.2 %copy-start.7 = (f32[4096]{0:T(1024)S(1)}, f32[4096]{0:T(1024)}, u32[]{:S(2)}) copy-start(f32[4096]{0:T(1024)} %param.18) | copy-start | bytes 49156
  351.1 252.3 %copy-start.2 = (bf16[128,1792]{1,0:T(8,128)(2,1)S(1)}, bf16[128,1792]{1,0:T(8,128)(2,1)}, u32[]{:S(2)}) copy-start(bf16[128,1792]{1,0:T(8,128)(2,1)} %param.22) | copy-start | bytes 1376260
  351.1 252.3 %copy-start.3 = (bf16[128,4096]{1,0:T(8,128)(2,1)S(1)}, bf16[128,4096]{1,0:T(8,128)(2,1)}, u32[]{:S(2)}) copy-start(bf16[128,4096]{1,0:T(8,128)(2,1)} %all-gather.5.cloned.1.call-done) | copy-start | bytes 3145732
  358.9 253.6 %copy-start.1 = (f32[128,1792]{1,0:T(8,128)}, f32[128,1792]{1,0:T(8,128)S(1)}, u32[]{:S(2)}) copy-start(f32[128,1792]{1,0:T(8,128)S(1)} %convolution_maximum_fusion) | copy-start | bytes 2752516
  612.5 107.9 %reduce-scatter.5.cloned.1.call-start = ((), (), s32[]{:S(2)}) async-start(), calls=%async_computation.8 | async-start | bytes 1310720 | tf_op jit(solution)/shard_map/reduce_scatter | solution.py:130
  634.9 92.3 %reduce-scatter.3.cloned.1.call-start = ((), (), s32[]{:S(2)}) async-start(), calls=%async_computation.7 | async-start | bytes 1310720 | tf_op jit(solution)/shard_map/reduce_scatter | solution.py:100
  684.9 35.5 %copy-start = (bf16[128,1024]{1,0:T(8,128)(2,1)S(1)}, bf16[128,1024]{1,0:T(8,128)(2,1)}, u32[]{:S(2)}) copy-start(bf16[128,1024]{1,0:T(8,128)(2,1)} %add_convert_fusion) | copy-start | bytes 786436
Sparse Core Ops, SparseCore 0:
  78.2 18.8 all-gather.4
  98.6 252.4 all-gather.6
  352.7 250.6 all-gather.8
  612.6 39.5 all-gather.10
  654.5 23.6 reduce-scatter.4
  686.2 23.9 reduce-scatter.2
where the time goes:
time: 738 us; the launch traced here: 737 us
  waiting for transfers between devices  554 us (75%)
  blocking collectives  65.6 us (9%)
  matrix products  49.4 us (7%)
  starting transfers between devices  36 us (5%)
  between operations  17.5 us (2%)
  other arithmetic  8.21 us (1%)
    all_gather x1, waiting for transfers between devices, local(): lax.all_gather(w_gate, 'ctx', axis=0, tiled=True)  253 us
    all_gather x1, waiting for transfers between devices, local(): lax.all_gather(w_up, 'ctx', axis=0, tiled=True)  245 us
    ppermute x8, starting transfers between devices, passed_along(): return lax.ppermute(block, axis, route)  35.6 us
    psum x1, blocking collectives, local(): lax.psum((loss_part, count_part), ('ctx', 'head', 'pair'))  31.7 us
    all_to_all x1, blocking collectives, local(): lax.all_to_all(local_part, 'ctx', split_axis=0, concat_axis=1, tiled=True)  28.1 us
    ppermute x8, waiting for transfers between devices, passed_along(): return lax.ppermute(block, axis, route)  21.8 us
    all_gather x1, waiting for transfers between devices, local(): all_hidden = lax.all_gather(hidden, 'ctx', axis=0, tiled=True)  17.2 us
    all_gather x1, waiting for transfers between devices, local(): gathered = lax.all_gather(residual, ('head', 'pair'), axis=1, tiled=True)  16.9 us
  transfers between devices with their start and end apart: 14, of which 12 were waited for; matrix products, arithmetic and copies ran while one was open for 5% of the time, Pallas kernels for 0%

commit v1 on v0

--- a/solution.py
+++ b/solution.py
@@ -84,7 +84,9 @@
     normed = (full_float / rms_value * norm_gain).astype(jnp.bfloat16)
     gate_full, up_full = (
         lax.all_gather(w_gate, "ctx", axis=0, tiled=True),
-        lax.all_gather(w_up, "ctx", axis=0, tiled=True),
+        jnp.concatenate(
+            lax.all_to_all(jnp.stack([w_up] * lax.axis_size("ctx")), "ctx", 0, 0), axis=0
+        ),
     )
     gate_proj = jnp.dot(normed, gate_full, preferred_element_type=jnp.float32)
     up_proj = jnp.dot(normed, up_full, preferred_element_type=jnp.float32)

time: 738 us -> 774 us (1.049)
  waiting for transfers between devices: 554 us -> 577 us
    all_gather x1, waiting for transfers between devices: 253 us -> 502 us  [local(): lax.all_gather(w_gate, 'ctx', axis=0, tiled=True)]
    all_gather x1 -> x0, waiting for transfers between devices: 245 us -> none  [local(): lax.all_gather(w_up, 'ctx', axis=0, tiled=True)]
    all_to_all x0 -> x1, waiting for transfers between devices: none -> 30.2 us  [local(): lax.all_to_all(jnp.stack([w_up] * lax.axis_size('ctx')), 'ctx', 0, 0)]
    all_gather x1, waiting for transfers between devices: 16.9 us -> 4.17 us  [local(): gathered = lax.all_gather(residual, ('head', 'pair'), axis=1, tiled=True)]
  transfers between devices with their start and end apart: 14 -> 14, of which waited for: 12 -> 12; matrix products, arithmetic and copies ran while one was open for 5% -> 6% of each run, Pallas kernels for 0% -> 0%
where the time goes in v1:
time: 774 us; the launch traced here: 773 us
  waiting for transfers between devices  577 us (75%)
  blocking collectives  65.6 us (8%)
  matrix products  49.3 us (6%)
  starting transfers between devices  42.8 us (6%)
  between operations  17.2 us (2%)
  local copies, waits for them, and re-layouts  12.6 us (2%)
  other arithmetic  8.21 us (1%)
    all_gather x1, waiting for transfers between devices, local(): lax.all_gather(w_gate, 'ctx', axis=0, tiled=True)  502 us
    ppermute x8, starting transfers between devices, passed_along(): return lax.ppermute(block, axis, route)  35.6 us
    psum x1, blocking collectives, local(): lax.psum((loss_part, count_part), ('ctx', 'head', 'pair'))  31.7 us
    all_to_all x1, waiting for transfers between devices, local(): lax.all_to_all(jnp.stack([w_up] * lax.axis_size('ctx')), 'ctx', 0, 0)  30.2 us
    all_to_all x1, blocking collectives, local(): lax.all_to_all(local_part, 'ctx', split_axis=0, concat_axis=1, tiled=True)  28.1 us
    ppermute x8, waiting for transfers between devices, passed_along(): return lax.ppermute(block, axis, route)  21.8 us
    all_gather x1, waiting for transfers between devices, local(): all_hidden = lax.all_gather(hidden, 'ctx', axis=0, tiled=True)  18 us
  transfers between devices with their start and end apart: 14, of which 12 were waited for; matrix products, arithmetic and copies ran while one was open for 6% of the time, Pallas kernels for 0%

profile of v1, /device:TPU:0, one launch (start us, length us, event | category | flops | bytes accessed | tf_op | source)
XLA Modules:
  0.0 773.1 jit_solution(7163228802819072010)
XLA Ops:
  7.2 0.1 add_bitcast_fusion
  7.3 0.1 broadcast_compare_fusion
  7.4 0.9 fusion.71
  8.3 57.8 %while.12 = (s32[]{:T(128)}, bf16[2,128,256]{2,1,0:T(8,128)(2,1)S(1)}, bf16[8,2,128,256]{3,2,1,0:T(8,128)(2,1)S(1)}, s32[]{:T(128)}) while((s32[]{:T(128)}, bf16[2,128,256]{2,1,0:T(8,128)(2,1)S(1)}, bf16[8,2,128,256]{3,2,1,0:T(8,128)(2,1)S(1)}, s32[]{:T(128)}) %tuple.30), condition=%wide.region_1.2_spmd, body=%wide.region_0.1_spmd.sunk | while | flops 2 | bytes 1048681 | solution.py:55
  8.3 5.0 collective-permute-start
  13.3 2.7 collective-permute-done
  16.0 4.4 collective-permute-start
  20.4 2.5 collective-permute-done
  23.0 4.4 collective-permute-start
  27.4 2.5 collective-permute-done
  29.9 4.4 collective-permute-start
  34.3 2.5 collective-permute-done
  36.8 4.4 collective-permute-start
  41.2 3.5 collective-permute-done
  44.8 4.4 collective-permute-start
  49.2 3.0 collective-permute-done
  52.3 4.4 collective-permute-start
  56.7 2.5 collective-permute-done
  59.2 4.4 collective-permute-start
  63.6 2.5 collective-permute-done
  66.1 0.1 fusion.25
  66.2 0.1 reshape_squeeze.7
  66.4 0.9 fusion.76
  67.3 0.1 copy-done.4
  67.3 0.2 copy.24
  67.5 0.9 fusion.27
  68.4 0.6 fusion.80
  69.0 0.6 fusion.79
  69.6 0.6 fusion.78
  70.2 0.6 fusion.77
  70.8 0.1 reshape_squeeze.6
  70.9 0.9 fusion.75
  71.8 0.6 copy.42
  72.5 0.8 convolution_bitcast_fusion.3
  73.3 0.8 convolution_bitcast_fusion.2
  74.1 0.6 copy.46
  74.7 0.8 convolution_bitcast_fusion.1
  75.5 0.8 convolution_bitcast_fusion
  76.4 0.2 copy.35
  76.6 0.7 copy-done.5
  77.3 0.8 add_convert_fusion
  78.1 0.7 all-gather.6.cloned.1.call-update
  78.8 6.6 stack.19
  85.4 6.8 all-to-all-start
  92.2 0.2 all-gather.8.cloned.1.call-start
  92.5 0.1 broadcast_in_dim.67
  92.6 0.3 copy.37
  92.9 4.2 all-gather.4.cloned.1.call-done
  97.1 1.5 fusion.21
  98.6 502.1 %all-gather.6.cloned.1.call-done = bf16[4096,1792]{1,0:T(8,128)(2,1)} async-done(((bf16[1024,1792]{1,0:T(8,128)(2,1)}), bf16[4096,1792]{1,0:T(8,128)(2,1)}) %all-gather.6.cloned.1.call-update) | async-done | bytes 14680080 | tf_op jit(solution)/shard_map/all_gather | solution.py:86
  600.7 7.7 convolution_maximum_fusion
  608.4 30.2 %all-to-all-done = bf16[4,1024,1792]{2,1,0:T(8,128)(2,1)} async-done(((bf16[4,1024,1792]{2,1,0:T(8,128)(2,1)}), bf16[4,1024,1792]{2,1,0:T(8,128)(2,1)}, u32[]{:S(2)}, u32[]{:S(2)}) %all-to-all-start) | async-done | bytes 14680096 | tf_op jit(solution)/shard_map/all_to_all | solution.py:88
  638.7 9.0 %multiply_reduce_fusion = (f32[]{:T(128)}, bf16[128,1792]{1,0:T(8,128)(2,1)}, f32[128,1792]{1,0:T(8,128)}) fusion(bf16[128,1792]{1,0:T(8,128)(2,1)S(1)} %copy-done.2, f32[128,1792]{1,0:T(8,128)S(1)} %copy.37, f32[128,1792]{1,0:T(8,128)S(1)} %convolution_maximum_fusion, bf16[4096,1792]{1,0:T(8,128)(2,1)} %bitcast.27, bf16[128,4096]{1,0:T(8,128)(2,1)S(1)} %copy-done.3, ...), kind=kOutput, calls=%fused_computation.46 | convolution fusion | flops 1882980352 | bytes 19415556 | tf_op jit(solution)/shard_map/dot_general | solution.py:92
  647.8 10.6 %fusion.32 = f32[128,4096]{1,0:T(8,128)S(1)} fusion(bf16[4096,1792]{1,0:T(8,128)(2,1)} %all-gather.6.cloned.1.call-done, f32[128,1792]{1,0:T(8,128)} %copy-done.1, f32[128,1792]{1,0:T(8,128)} %get-tuple-element.43, f32[128,1792]{1,0:T(8,128)S(1)} %copy.37, bf16[128,1792]{1,0:T(8,128)(2,1)S(1)} %copy-done.2), kind=kOutput, calls=%fused_computation.66 | convolution fusion | flops 1881112576 | bytes 19988480 | tf_op jit(solution)/shard_map/dot_general | solution.py:124
  658.4 11.6 %fusion.4 = bf16[128,4096]{1,0:T(8,128)(2,1)} fusion(f32[128,4096]{1,0:T(8,128)S(1)} %fusion.32, bf16[4096,1792]{1,0:T(8,128)(2,1)} %bitcast.27, f32[128,1792]{1,0:T(8,128)} %copy-done.1, f32[128,1792]{1,0:T(8,128)S(1)} %copy.37, bf16[128,1792]{1,0:T(8,128)(2,1)S(1)} %copy-done.2, f32[128,1792]{1,0:T(8,128)} %get-tuple-element.43), kind=kOutput, calls=%fused_computation.6 | convolution fusion | flops 1881702400 | bytes 21037056 | tf_op jit(solution)/shard_map/dot_general | solution.py:125
  670.1 18.0 %all-gather.8.cloned.1.call-done = bf16[512,1792]{1,0:T(8,128)(2,1)} async-done(((bf16[128,1792]{1,0:T(8,128)(2,1)}), bf16[512,1792]{1,0:T(8,128)(2,1)}) %all-gather.8.cloned.1.call-update) | async-done | bytes 1835024 | tf_op jit(solution)/shard_map/all_gather | solution.py:97
  688.1 4.7 convolution_convert_fusion
  692.8 28.1 %all_to_all.24 = bf16[4,128,1024]{2,1,0:T(8,128)(2,1)S(1)} all-to-all(bf16[4,128,1024]{2,1,0:T(8,128)(2,1)S(1)} %bitcast.217), channel_id=1, replica_groups=mesh['groups'=2,'ctx'=4,'head'=2,'pair'=2] {'ctx'}, dimensions={0} | all-to-all | bytes 2097152 | tf_op jit(solution)/shard_map/all_to_all | solution.py:101
  720.9 1.1 copy.50
  722.0 0.6 convert_reduce_fusion
  723.3 31.7 %all-reduce = (f32[]{:T(128)}, f32[]{:T(128)}) all-reduce(f32[]{:T(128)} %get-tuple-element.29, f32[]{:T(128)S(6)} %mul.149), channel_id=1, replica_groups=mesh['groups'=2,'ctx'=4,'head'=2,'pair'=2] {'ctx','head','pair'}, use_global_device_ids=true, to_apply=%region_13.14 | all-reduce | flops 2 | bytes 16 | tf_op jit(solution)/shard_map/psum | solution.py:118
  756.4 1.1 fusion.29
  757.5 5.8 psum.23
  763.3 2.1 fusion.31
  (49 shorter events, 0.6 us)
Async XLA Ops:
  7.2 89.9 %all-gather.4.cloned.1.call-start = ((), (), s32[]{:S(2)}) async-start(), calls=%async_computation.4 | async-start | bytes 1310720 | tf_op jit(solution)/shard_map/all_gather | solution.py:81
  8.3 7.7 collective-permute-start
  16.0 6.9 collective-permute-start
  23.0 6.9 collective-permute-start
  29.9 6.9 collective-permute-start
  36.8 7.9 %collective-permute-start = (bf16[2,128,256]{2,1,0:T(8,128)(2,1)S(1)}, bf16[2,128,256]{2,1,0:T(8,128)(2,1)S(1)}, u32[]{:S(2)}, u32[]{:S(2)}) collective-permute-start(bf16[2,128,256]{2,1,0:T(8,128)(2,1)S(1)} %get-tuple-element.68), channel_id=1, source_target_pairs={{0,4},{4,8},{8,12},{1,5},{5,9},{9,13},{2,6},{6,10},{10,14},{3,7},{... | collective-permute-start | bytes 393224 | tf_op jit(solution)/shard_map/while/body/eval_jaxpr/ppermute | solution.py:18
  44.8 7.4 collective-permute-start
  52.3 6.9 collective-permute-start
  59.2 6.9 collective-permute-start
  66.4 1.0 copy-start.4
  66.4 1.1 copy-start.8
  76.3 1.0 copy-start.5
  78.1 522.6 %all-gather.6.cloned.1.call-start = ((), (), s32[]{:S(2)}) async-start(), calls=%async_computation.5 | async-start | bytes 18350080 | tf_op jit(solution)/shard_map/all_gather | solution.py:86
  85.4 7.1 copy-start.6
  85.4 553.2 %all-to-all-start = ((bf16[4,1024,1792]{2,1,0:T(8,128)(2,1)}), bf16[4,1024,1792]{2,1,0:T(8,128)(2,1)}, u32[]{:S(2)}, u32[]{:S(2)}) async-start(bf16[4,1024,1792]{2,1,0:T(8,128)(2,1)} %stack.19), calls=%async_computation | async-start | bytes 29360128 | tf_op jit(solution)/shard_map/all_to_all | solution.py:88
  92.2 595.9 %all-gather.8.cloned.1.call-start = ((), (), s32[]{:S(2)}) async-start(), calls=%async_computation.6 | async-start | bytes 2293760 | tf_op jit(solution)/shard_map/all_gather | solution.py:97
  92.6 508.1 %copy-start.7 = (f32[4096]{0:T(1024)S(1)}, f32[4096]{0:T(1024)}, u32[]{:S(2)}) copy-start(f32[4096]{0:T(1024)} %param.18) | copy-start | bytes 49156
  600.7 38.0 %copy-start.2 = (bf16[128,1792]{1,0:T(8,128)(2,1)S(1)}, bf16[128,1792]{1,0:T(8,128)(2,1)}, u32[]{:S(2)}) copy-start(bf16[128,1792]{1,0:T(8,128)(2,1)} %param.22) | copy-start | bytes 1376260
  600.7 38.0 %copy-start.3 = (bf16[128,4096]{1,0:T(8,128)(2,1)S(1)}, bf16[128,4096]{1,0:T(8,128)(2,1)}, u32[]{:S(2)}) copy-start(bf16[128,4096]{1,0:T(8,128)(2,1)} %all-gather.4.cloned.1.call-done) | copy-start | bytes 3145732
  608.4 39.3 %copy-start.1 = (f32[128,1792]{1,0:T(8,128)}, f32[128,1792]{1,0:T(8,128)S(1)}, u32[]{:S(2)}) copy-start(f32[128,1792]{1,0:T(8,128)S(1)} %convolution_maximum_fusion) | copy-start | bytes 2752516
  647.7 108.7 %reduce-scatter.5.cloned.1.call-start = ((), (), s32[]{:S(2)}) async-start(), calls=%async_computation.8 | async-start | bytes 1310720 | tf_op jit(solution)/shard_map/reduce_scatter | solution.py:132
  670.1 93.2 %reduce-scatter.3.cloned.1.call-start = ((), (), s32[]{:S(2)}) async-start(), calls=%async_computation.7 | async-start | bytes 1310720 | tf_op jit(solution)/shard_map/reduce_scatter | solution.py:102
  720.9 35.5 %copy-start = (bf16[128,1024]{1,0:T(8,128)(2,1)S(1)}, bf16[128,1024]{1,0:T(8,128)(2,1)}, u32[]{:S(2)}) copy-start(bf16[128,1024]{1,0:T(8,128)(2,1)} %add_convert_fusion) | copy-start | bytes 786436
Sparse Core Ops, SparseCore 0:
  78.2 18.8 all-gather.3
  98.6 501.9 all-gather.5
  647.8 40.2 all-gather.7
  690.5 23.6 reduce-scatter.4
  722.1 23.9 reduce-scatter.2
